TPU v7x, 256 devices: a whole 4x4x8 slice. The times are simulated.
256 devices in a mesh: tok: 64 (over x, z, core), feat: 4 (over y).
Axes of the slice: x: 4, y: 4, z: 8, core: 2. Of those that a mesh axis runs over, the one named last changes fastest.
Arguments:
- queries: bfloat16 [8192, 4096], P('tok', 'feat'), may hold values from -12 to 12
- keys: bfloat16 [8192, 1024], P('tok', 'feat'), may hold values from -12 to 12
- values: bfloat16 [8192, 1024], P('tok', 'feat'), may hold values from -6 to 6
- out_weight: bfloat16 [4096, 4096], P('feat', 'tok'), may hold values from -0.09375 to 0.09375
- doc_lengths: int32 [6], replicated, may hold values from 1 to 5120, 8192 in all
Outputs:
- mixed: bfloat16 [8192, 4096], P('tok', 'feat')
Inputs may be any that keep to these rules, and one draw needn't show every extreme that they name: `doc_lengths`: the lengths sum to 8192, and the largest is exactly 5120.
All inputs are finite; a program needn't handle non-finite values.
Results may differ from a plain program's by a relative error of at most 0.012.
The roundings to bfloat16 on the way count: a program that leaves them out, or rounds other values in their place, can miss the bound.
Values may be sent and summed in bfloat16 or wider, within the bound.
A program may use at most 64 MiB of HBM per device.

v0:
```python
import jax
import jax.numpy as jnp
from jax import lax
from jax.sharding import PartitionSpec as P

HD = 128
ROPE_BASE = 500000.0
NEG_FILL = -1e30


def locate(token_index, doc_lengths):
    doc_ends = jnp.cumsum(doc_lengths)
    starts = doc_ends - doc_lengths
    doc_ids = jnp.sum((token_index[:, None] >= doc_ends[None, :]).astype(jnp.int32), axis=1)
    number = jnp.arange(doc_lengths.shape[0], dtype=jnp.int32)
    first_token = jnp.sum(
        jnp.where(doc_ids[:, None] == number[None, :], starts[None, :], 0), axis=1
    )
    return (doc_ids, token_index - first_token)


def rotary(tensor, positions):
    half_size = tensor.shape[-1] // 2
    frequency = ROPE_BASE ** (-(jnp.arange(half_size, dtype=jnp.float32) * 2.0 / tensor.shape[-1]))
    angles = positions.astype(jnp.float32)[:, None] * frequency[None, :]
    cosine = jnp.cos(angles)[:, None, :]
    sine_part = jnp.sin(angles)[:, None, :]
    first_half = tensor[..., :half_size]
    second_half = tensor[..., half_size:]
    return jnp.concatenate(
        [
            first_half * cosine - second_half * sine_part,
            second_half * cosine + first_half * sine_part,
        ],
        axis=-1,
    )


def pick_block(extent):
    for candidate in (512, 256, 128):
        return candidate
    return extent


def shards(queries, keys, values, out_weight, doc_lengths):
    my_index = lax.axis_index("tok")
    local_rows = queries.shape[0]
    local_heads = queries.shape[1] // HD
    kv_local = keys.shape[1] // HD
    group_size = local_heads // kv_local
    scale_factor = HD ** (-0.5)
    own_index = my_index * local_rows + jnp.arange(local_rows, dtype=jnp.int32)
    own_docs, own_positions = locate(own_index, doc_lengths)
    rotated_q = rotary(
        queries.astype(jnp.float32).reshape(local_rows, local_heads, HD), own_positions
    ).astype(jnp.bfloat16)
    rotated_k = rotary(
        keys.astype(jnp.float32).reshape(local_rows, kv_local, HD), own_positions
    ).astype(jnp.bfloat16)
    rotated_k = rotated_k.reshape(local_rows, kv_local * HD)

    def fresh(query_rows):
        running_max = jnp.full((kv_local, group_size, query_rows), NEG_FILL, jnp.float32)
        totals = jnp.zeros((kv_local, group_size, query_rows), jnp.float32)
        weighted = jnp.zeros((kv_local, group_size, query_rows, HD), jnp.float32)
        return (running_max, totals, weighted)

    def absorb(carry_state, query_block, query_index, key_piece, value_piece, offset):
        query_docs, query_positions = locate(query_index, doc_lengths)
        doc_begin = query_index[0] - query_positions[0]
        last_index = query_index[-1]
        extent = key_piece.shape[0]
        needed = (offset + extent > doc_begin) & (offset <= last_index)
        block_rows = pick_block(extent)

        def sweep_keys(state_in):

            def one_block(block_number, state_now):
                running_max, totals, weighted = state_now
                first_key = block_number * block_rows
                key_tile = lax.dynamic_slice_in_dim(key_piece, first_key, block_rows, 0).reshape(
                    block_rows, kv_local, HD
                )
                value_tile = lax.dynamic_slice_in_dim(
                    value_piece, first_key, block_rows, 0
                ).reshape(block_rows, kv_local, HD)
                key_index = first_key + jnp.arange(block_rows, dtype=jnp.int32)
                key_docs, key_positions = locate(key_index, doc_lengths)
                scores = (
                    jnp.einsum(
                        "qgjd,kgd->gjqk", query_block, key_tile, preferred_element_type=jnp.float32
                    )
                    * scale_factor
                )
                visible = (query_docs[:, None] == key_docs[None, :]) & (
                    key_index[None, :] <= query_index[:, None]
                )
                scores = jnp.where(visible, scores, NEG_FILL)
                new_max = jnp.maximum(running_max, jnp.max(scores, axis=-1))
                factor = jnp.exp(running_max - new_max)
                weights = jnp.where(visible, jnp.exp(scores - new_max[..., None]), 0.0)
                totals = totals * factor + jnp.sum(weights, axis=-1)
                update = jnp.einsum(
                    "gjqk,kgd->gjqd",
                    weights.astype(jnp.bfloat16),
                    value_tile,
                    preferred_element_type=jnp.float32,
                )
                weighted = weighted * factor[..., None] + update
                return (new_max, totals, weighted)

            return lax.fori_loop(0, extent // block_rows, one_block, state_in)

        return lax.cond(needed, sweep_keys, lambda state_in: state_in, carry_state)

    def finish(carry_state):
        running_max, totals, weighted = carry_state
        output = weighted / totals[..., None]
        query_rows = output.shape[2]
        return (
            output.transpose(2, 0, 1, 3).reshape(query_rows, local_heads * HD).astype(jnp.bfloat16)
        )

    groups = [(rotated_q, own_index)]
    query_sets = [
        (member[0].reshape(member[0].shape[0], kv_local, group_size, HD), member[1])
        for member in groups
    ]

    def fold_keys(states, pieces, offset):
        return tuple(
            (
                absorb(state_now, member[0], member[1], pieces[0], pieces[1], offset)
                for state_now, member in zip(states, query_sets)
            )
        )

    initial = tuple((fresh(member[0].shape[0]) for member in query_sets))
    states = fold_keys(
        initial,
        (
            lax.all_gather(rotated_k, "tok", axis=0, tiled=True),
            lax.all_gather(values, "tok", axis=0, tiled=True),
        ),
        jnp.int32(0),
    )
    results = [finish(state_now) for state_now in states]
    attended = results[0]
    partial_terms = jnp.dot(
        attended,
        lax.all_gather(out_weight, "tok", axis=1, tiled=True),
        preferred_element_type=jnp.float32,
    )
    return lax.psum_scatter(
        partial_terms.astype(jnp.bfloat16), "feat", scatter_dimension=1, tiled=True
    )


def solution(mesh):
    in_specs = (P("tok", "feat"), P("tok", "feat"), P("tok", "feat"), P("feat", "tok"), P())
    out_specs = P("tok", "feat")
    return jax.shard_map(shards, mesh=mesh, in_specs=in_specs, out_specs=out_specs, check_vma=False)
```

profile of v0, /device:TPU:2, one launch (start us, length us, event | category | flops | bytes accessed | tf_op | source)
XLA Modules:
  0.0 290.6 jit_solution(7119460857731323404)
XLA Ops:
  10.1 1.6 copy.40
  16.3 73.4 %all-gather.4.cloned.1.call-done = bf16[8192,256]{0,1:T(8,128)(2,1)} async-done(((bf16[128,256]{0,1:T(8,128)(2,1)}), bf16[8192,256]{0,1:T(8,128)(2,1)}) %all-gather.4.cloned.1.call-update) | async-done | bytes 4194320 | tf_op jit(solution)/shard_map/all_gather | solution.py:142
  89.7 78.3 %all-gather.6.cloned.1.call-done = bf16[8192,256]{0,1:T(8,128)(2,1)} async-done(((bf16[128,256]{0,1:T(8,128)(2,1)}), bf16[8192,256]{0,1:T(8,128)(2,1)}) %all-gather.6.cloned.1.call-update) | async-done | bytes 4194320 | tf_op jit(solution)/shard_map/all_gather | solution.py:143
  168.0 75.7 %conditional.1 = (f32[2,4,128]{2,1,0:T(4,128)}, f32[2,4,128,128]{2,3,1,0:T(8,128)S(1)}) conditional(s32[]{:T(128)} %bitcast.3, () %tuple.34, (s32[6]{0:T(128)S(1)}, s32[128]{0:T(128)S(1)}, s32[128]{0:T(128)S(1)}, bf16[8192,256]{0,1:T(8,128)(2,1)}, bf16[128,2,4,128]{3,0,2,1:T(8,128)(2,1)S(1)}, /*index=5*/bf16[8192,256]{0,1:T(8,128)(2,1)}) %tuple.78), branch_computations={%region_3.4_spmd, %region_4.11_spmd} | conditional | flops 275855392 | bytes 10562971 | solution.py:114
  168.2 75.3 %while.19 = (s32[]{:T(128)}, f32[2,4,128]{2,1,0:T(4,128)S(1)}, f32[2,4,128]{2,1,0:T(4,128)}, f32[2,4,128,128]{3,2,1,0:T(8,128)S(1)}, s32[128]{0:T(128)S(1)}, /*i...) while((s32[]{:T(128)}, f32[2,4,128]{2,1,0:T(4,128)S(1)}, ...), condition=%wide.region_10.10_spmd.clone, body=%wide.region_6.9_spmd.clone.sunk | while | flops 275855360 | bytes 9514207 | solution.py:112
  174.7 1.3 fusion.35
  177.0 1.1 constant_dynamic-slice_fusion.3
  179.5 1.3 fusion.35
  181.8 1.1 constant_dynamic-slice_fusion.3
  184.2 1.3 fusion.35
  186.5 1.1 constant_dynamic-slice_fusion.3
  189.0 1.3 fusion.35
  191.3 1.1 constant_dynamic-slice_fusion.3
  193.7 1.3 fusion.35
  196.0 1.1 constant_dynamic-slice_fusion.3
  198.5 1.3 fusion.35
  203.2 1.3 fusion.35
  205.5 1.1 constant_dynamic-slice_fusion.3
  208.0 1.3 fusion.35
  212.7 1.3 fusion.35
  217.4 1.3 fusion.35
  219.7 1.1 constant_dynamic-slice_fusion.3
  222.2 1.3 fusion.35
  227.0 1.3 fusion.35
  229.2 1.1 constant_dynamic-slice_fusion.3
  231.7 1.3 fusion.35
  234.0 1.2 constant_dynamic-slice_fusion.3
  236.6 1.3 fusion.35
  241.3 1.3 fusion.35
  244.5 7.3 %all-gather.8.cloned.1.call-done = bf16[1024,4096]{0,1:T(8,128)(2,1)} async-done(((bf16[1024,64]{0,1:T(8,128)(2,1)}), bf16[1024,4096]{0,1:T(8,128)(2,1)}) %all-gather.8.cloned.1.call-update) | async-done | bytes 8388624 | tf_op jit(solution)/shard_map/all_gather | solution.py:151
  251.8 7.3 %convolution_convert_fusion = bf16[128,4096]{1,0:T(8,128)(2,1)} fusion(bf16[128,1024]{0,1:T(8,128)(2,1)S(1)} %bitcast.64, bf16[1024,4096]{0,1:T(8,128)(2,1)} %all-gather.8.cloned.1.call-done), kind=kOutput, calls=%fused_computation.23 | convolution fusion | flops 1074266112 | bytes 9699328 | tf_op jit(solution)/shard_map/dot_general | solution.py:149
  259.1 24.9 %reduce-scatter.2.cloned.1.call-done = bf16[128,1024]{1,0:T(8,128)(2,1)} async-done(((bf16[128,4096]{1,0:T(8,128)(2,1)}), bf16[128,1024]{1,0:T(8,128)(2,1)}) %reduce-scatter.2.cloned.1.call-update) | async-done | bytes 262160 | tf_op jit(solution)/shard_map/reduce_scatter | solution.py:154
  (171 shorter events, 52.9 us)
Async XLA Ops:
  6.5 83.2 %all-gather.4.cloned.1.call-start = ((), (), s32[]{:S(2)}) async-start(), calls=%async_computation.1 | async-start | bytes 4259840 | tf_op jit(solution)/shard_map/all_gather | solution.py:142
  10.1 158.0 %all-gather.6.cloned.1.call-start = ((), (), s32[]{:S(2)}) async-start(), calls=%async_computation.2 | async-start | bytes 4259840 | tf_op jit(solution)/shard_map/all_gather | solution.py:143
  11.7 240.1 %all-gather.8.cloned.1.call-start = ((), (), s32[]{:S(2)}) async-start(), calls=%async_computation.3 | async-start | bytes 8519680 | tf_op jit(solution)/shard_map/all_gather | solution.py:151
  12.4 271.6 %reduce-scatter.2.cloned.1.call-start = ((), (), s32[]{:S(2)}) async-start(), calls=%async_computation.4 | async-start | bytes 1310720 | tf_op jit(solution)/shard_map/reduce_scatter | solution.py:154
  15.7 152.3 %copy-start = (s32[6]{0:T(128)S(1)}, s32[6]{0:T(128)}, u32[]{:S(2)}) copy-start(s32[6]{0:T(128)} %param.13) | copy-start | bytes 76
Sparse Core Ops, SparseCore 0:
  10.2 79.5 all-gather.3
  92.3 75.6 all-gather.5
  170.8 80.9 all-gather.7
  259.3 24.7 reduce-scatter.1
where the time goes:
time: 292 us; the launch traced here: 291 us
  waiting for transfers between devices  185 us (63%)
  other arithmetic  38.1 us (13%)
  matrix products  31 us (11%)
  local copies, waits for them, and re-layouts  21.2 us (7%)
  between operations  14.5 us (5%)
    all_gather x1, waiting for transfers between devices, shards(): lax.all_gather(values, 'tok', axis=0, tiled=True)  78.3 us
    all_gather x1, waiting for transfers between devices, shards(): lax.all_gather(rotated_k, 'tok', axis=0, tiled=True)  73.4 us
    reduce_scatter x1, waiting for transfers between devices, shards(): lax.psum_scatter(partial_terms.astype(jnp.bfloat16), 'feat', scatter_dime...  24.9 us
    add x16, other arithmetic, one_block(): totals = totals * factor + jnp.sum(weights, axis=-1)  20.1 us
    dynamic_slice x16, local copies, waits for them, and re-layouts, one_block(): lax.dynamic_slice_in_dim(value_piece, first_key, block_rows, 0)  17.3 us
    dot_general x16, matrix products, one_block(): jnp.einsum('gjqk,kgd->gjqd', weights.astype(jnp.bfloat16), value_tile, pr...  15.1 us
    dot_general x16, matrix products, one_block(): jnp.einsum('qgjd,kgd->gjqk', query_block, key_tile, preferred_element_typ...  8.59 us
    reduce_sum x16, other arithmetic, one_block(): totals = totals * factor + jnp.sum(weights, axis=-1)  8.35 us
  transfers between devices with their start and end apart: 4, of which 4 were waited for; matrix products, arithmetic and copies ran while one was open for 27% of the time, Pallas kernels for 0%

commit v1 on v0

--- a/solution.py
+++ b/solution.py
@@ -1,11 +1,22 @@
+import functools
 import jax
 import jax.numpy as jnp
 from jax import lax
 from jax.sharding import PartitionSpec as P
+from jax.lax import all_to_all, axis_size
 
 HD = 128
 ROPE_BASE = 500000.0
 NEG_FILL = -1e30
+
+
+def supply_all_the_signs(unit, dim_no):
+    raw_out = jnp.stack([unit for _ in range(axis_size("tok"))], 0)
+    built = all_to_all(raw_out, "tok", 0, 0)
+    return jnp.concatenate(built, dim_no)
+
+
+things_unite = functools.partial(supply_all_the_signs, dim_no=0)
 
 
 def locate(token_index, doc_lengths):
@@ -138,10 +149,7 @@
     initial = tuple((fresh(member[0].shape[0]) for member in query_sets))
     states = fold_keys(
         initial,
-        (
-            lax.all_gather(rotated_k, "tok", axis=0, tiled=True),
-            lax.all_gather(values, "tok", axis=0, tiled=True),
-        ),
+        (lax.all_gather(rotated_k, "tok", axis=0, tiled=True), things_unite(values)),
         jnp.int32(0),
     )
     results = [finish(state_now) for state_now in states]

time: 292 us -> 258 us (0.88)
  waiting for transfers between devices: 185 us -> 132 us
  starting transfers between devices: 0.12 us -> 12.4 us
  local copies, waits for them, and re-layouts: 21.2 us -> 28.2 us
    all_gather x1 -> x0, waiting for transfers between devices: 78.3 us -> none  [shards(): lax.all_gather(values, 'tok', axis=0, tiled=True)]
    all_gather x1, waiting for transfers between devices: 73.4 us -> 102 us  [shards(): lax.all_gather(rotated_k, 'tok', axis=0, tiled=True)]
    all_to_all x0 -> x1, starting transfers between devices: none -> 12.3 us  [supply_all_the_signs(): built = all_to_all(raw_out, 'tok', 0, 0)]
    reshape x0 -> x1, local copies, waits for them, and re-layouts: none -> 4.76 us  [supply_all_the_signs(): return jnp.concatenate(built, dim_no)]
    all_gather x1, waiting for transfers between devices: 7.27 us -> 2.65 us  [shards(): lax.all_gather(out_weight, 'tok', axis=1, tiled=True)]
    another operation x0 -> x1, local copies, waits for them, and re-layouts: none -> 2.95 us  [supply_all_the_signs(): raw_out = jnp.stack([unit for _ in range(axis_size('tok'))], 0)]
  transfers between devices with their start and end apart: 4 -> 4, of which waited for: 4 -> 4; matrix products, arithmetic and copies ran while one was open for 27% -> 33% of each run, Pallas kernels for 0% -> 0%
where the time goes in v1:
time: 258 us; the launch traced here: 256 us
  waiting for transfers between devices  132 us (51%)
  other arithmetic  37.2 us (14%)
  matrix products  31.1 us (12%)
  local copies, waits for them, and re-layouts  28.2 us (11%)
  between operations  14.5 us (6%)
  starting transfers between devices  12.4 us (5%)
    all_gather x1, waiting for transfers between devices, shards(): lax.all_gather(rotated_k, 'tok', axis=0, tiled=True)  102 us
    reduce_scatter x1, waiting for transfers between devices, shards(): lax.psum_scatter(partial_terms.astype(jnp.bfloat16), 'feat', scatter_dime...  24.9 us
    add x16, other arithmetic, one_block(): totals = totals * factor + jnp.sum(weights, axis=-1)  20.1 us
    dynamic_slice x16, local copies, waits for them, and re-layouts, one_block(): lax.dynamic_slice_in_dim(value_piece, first_key, block_rows, 0)  17.2 us
    dot_general x16, matrix products, one_block(): jnp.einsum('gjqk,kgd->gjqd', weights.astype(jnp.bfloat16), value_tile, pr...  15.1 us
    all_to_all x1, starting transfers between devices, supply_all_the_signs(): built = all_to_all(raw_out, 'tok', 0, 0)  12.3 us
    dot_general x16, matrix products, one_block(): jnp.einsum('qgjd,kgd->gjqk', query_block, key_tile, preferred_element_typ...  8.64 us
    reduce_sum x16, other arithmetic, one_block(): totals = totals * factor + jnp.sum(weights, axis=-1)  8.37 us
  transfers between devices with their start and end apart: 4, of which 4 were waited for; matrix products, arithmetic and copies ran while one was open for 33% of the time, Pallas kernels for 0%

profile of v1, /device:TPU:2, one launch (start us, length us, event | category | flops | bytes accessed | tf_op | source)
XLA Modules:
  0.0 256.5 jit_solution(6624826881953051217)
XLA Ops:
  11.8 3.0 %stack.2 = bf16[64,128,256]{1,2,0:T(8,128)(2,1)} broadcast(bf16[128,256]{0,1:T(8,128)(2,1)S(1)} %copy.47), dimensions={1,2} | broadcast | bytes 4259840 | tf_op jit(solution)/shard_map/stack | solution.py:14
  14.7 12.3 %all-to-all-start = ((bf16[64,128,256]{1,2,0:T(8,128)(2,1)}), bf16[64,128,256]{1,2,0:T(8,128)(2,1)}, u32[]{:S(2)}, u32[]{:S(2)}) async-start(bf16[64,128,256]{1,2,0:T(8,128)(2,1)} %stack.2), calls=%async_computation | async-start | bytes 8388608 | tf_op jit(solution)/shard_map/all_to_all | solution.py:15
  29.9 101.7 %all-gather.3.cloned.1.call-done = bf16[8192,256]{0,1:T(8,128)(2,1)} async-done(((bf16[128,256]{0,1:T(8,128)(2,1)}), bf16[8192,256]{0,1:T(8,128)(2,1)}) %all-gather.3.cloned.1.call-update) | async-done | bytes 4194320 | tf_op jit(solution)/shard_map/all_gather | solution.py:152
  131.6 2.1 all-to-all-done
  133.7 80.5 %conditional.1 = (f32[2,4,128]{2,1,0:T(4,128)}, f32[2,4,128,128]{2,3,1,0:T(8,128)S(1)}) conditional(s32[]{:T(128)} %bitcast.3, () %tuple.34, (bf16[64,128,256]{1,2,0:T(8,128)(2,1)}, s32[6]{0:T(128)S(1)}, s32[128]{0:T(128)S(1)}, s32[128]{0:T(128)S(1)}, bf16[8192,256]{0,1:T(8,128)(2,1)}, /*index=5*/bf16[128,2,4,128]{3,0,2,1:T(8,128)(2,1)S(1)}) %tuple.79), branch_computations={%region_3.4_spmd, %region_4.11_spmd} | conditional | flops 275855392 | bytes 18951580 | solution.py:125
  133.7 4.8 %copy_bitcast_fusion = bf16[8192,256]{0,1:T(8,128)(2,1)} fusion(bf16[64,128,256]{1,2,0:T(8,128)(2,1)} %get-tuple-element.307), kind=kLoop, calls=%fused_computation.23 | loop fusion | bytes 8388608 | tf_op jit(solution)/shard_map/reshape | solution.py:16
  138.7 75.4 %while.19 = (s32[]{:T(128)}, f32[2,4,128]{2,1,0:T(4,128)S(1)}, f32[2,4,128]{2,1,0:T(4,128)}, f32[2,4,128,128]{3,2,1,0:T(8,128)S(1)}, s32[128]{0:T(128)S(1)}, /*i...) while((s32[]{:T(128)}, f32[2,4,128]{2,1,0:T(4,128)S(1)}, ...), condition=%wide.region_10.10_spmd.clone, body=%wide.region_6.9_spmd.clone.sunk | while | flops 275855360 | bytes 9514207 | solution.py:123
  142.7 1.1 constant_dynamic-slice_fusion.3
  145.2 1.3 fusion.36
  147.5 1.1 constant_dynamic-slice_fusion.3
  150.0 1.3 fusion.36
  152.2 1.1 constant_dynamic-slice_fusion.3
  154.7 1.3 fusion.36
  159.5 1.3 fusion.36
  164.2 1.3 fusion.36
  169.0 1.3 fusion.36
  173.7 1.3 fusion.36
  178.5 1.3 fusion.36
  183.2 1.3 fusion.36
  185.5 1.1 constant_dynamic-slice_fusion.3
  188.0 1.3 fusion.36
  192.8 1.3 fusion.36
  195.0 1.1 constant_dynamic-slice_fusion.3
  197.5 1.3 fusion.36
  199.8 1.1 constant_dynamic-slice_fusion.3
  202.3 1.3 fusion.36
  207.0 1.3 fusion.36
  209.3 1.1 constant_dynamic-slice_fusion.3
  211.8 1.3 fusion.36
  215.0 2.6 %all-gather.5.cloned.1.call-done = bf16[1024,4096]{0,1:T(8,128)(2,1)} async-done(((bf16[1024,64]{0,1:T(8,128)(2,1)}), bf16[1024,4096]{0,1:T(8,128)(2,1)}) %all-gather.5.cloned.1.call-update) | async-done | bytes 8388624 | tf_op jit(solution)/shard_map/all_gather | solution.py:159
  217.7 7.3 %convolution_convert_fusion = bf16[128,4096]{1,0:T(8,128)(2,1)} fusion(bf16[128,1024]{0,1:T(8,128)(2,1)S(1)} %bitcast.69, bf16[1024,4096]{0,1:T(8,128)(2,1)} %all-gather.5.cloned.1.call-done), kind=kOutput, calls=%fused_computation.24 | convolution fusion | flops 1074266112 | bytes 9699328 | tf_op jit(solution)/shard_map/dot_general | solution.py:157
  225.0 24.9 %reduce-scatter.2.cloned.1.call-done = bf16[128,1024]{1,0:T(8,128)(2,1)} async-done(((bf16[128,4096]{1,0:T(8,128)(2,1)}), bf16[128,1024]{1,0:T(8,128)(2,1)}) %reduce-scatter.2.cloned.1.call-update) | async-done | bytes 262160 | tf_op jit(solution)/shard_map/reduce_scatter | solution.py:162
  (174 shorter events, 55.0 us)
Async XLA Ops:
  6.5 125.1 %all-gather.3.cloned.1.call-start = ((), (), s32[]{:S(2)}) async-start(), calls=%async_computation.2 | async-start | bytes 4259840 | tf_op jit(solution)/shard_map/all_gather | solution.py:152
  10.1 207.6 %all-gather.5.cloned.1.call-start = ((), (), s32[]{:S(2)}) async-start(), calls=%async_computation.3 | async-start | bytes 8519680 | tf_op jit(solution)/shard_map/all_gather | solution.py:159
  14.7 12.6 %copy-start = (bf16[128,1024]{1,0:T(8,128)(2,1)S(1)}, bf16[128,1024]{1,0:T(8,128)(2,1)}, u32[]{:S(2)}) copy-start(bf16[128,1024]{1,0:T(8,128)(2,1)} %param.9) | copy-start | bytes 786436
  14.7 119.0 %all-to-all-start = ((bf16[64,128,256]{1,2,0:T(8,128)(2,1)}), bf16[64,128,256]{1,2,0:T(8,128)(2,1)}, u32[]{:S(2)}, u32[]{:S(2)}) async-start(bf16[64,128,256]{1,2,0:T(8,128)(2,1)} %stack.2), calls=%async_computation | async-start | bytes 8388608 | tf_op jit(solution)/shard_map/all_to_all | solution.py:15
  27.1 222.9 %reduce-scatter.2.cloned.1.call-start = ((), (), s32[]{:S(2)}) async-start(), calls=%async_computation.4 | async-start | bytes 1310720 | tf_op jit(solution)/shard_map/reduce_scatter | solution.py:162
  29.3 104.4 %copy-start.1 = (s32[6]{0:T(128)S(1)}, s32[6]{0:T(128)}, u32[]{:S(2)}) copy-start(s32[6]{0:T(128)} %param.13) | copy-start | bytes 76
Sparse Core Ops, SparseCore 0:
  10.2 121.3 all-gather.2
  134.4 83.2 all-gather.4
  225.1 24.7 reduce-scatter.1
